TPU v7x, 32 devices: a whole 2x2x4 slice. The times are simulated.
32 devices in a mesh: items: 16 (over z, y, core), seq: 2 (over x).
Axes of the slice: x: 2, y: 2, z: 4, core: 2. Of those that a mesh axis runs over, the one named last changes fastest.
Arguments:
- tokens: bfloat16 [16, 1280, 1024], P('items', 'seq'), may hold values from -6 to 6
- cotangent: bfloat16 [16, 1280, 1024], P('items', 'seq'), may hold values from -6 to 6
- prompt_len: int32 [16], P('items'), may hold values from 150 to 600
- section_ids: int32 [16], P('items'), may hold values from 0 to 7
- section_table: bfloat16 [8, 1024], replicated, may hold values from -6 to 6
- w_query: bfloat16 [1024, 1024], P('items'), may hold values from -0.1875 to 0.1875
- w_key: bfloat16 [1024, 1024], P('items'), may hold values from -0.1875 to 0.1875
- w_value: bfloat16 [1024, 1024], P('items'), may hold values from -0.1875 to 0.1875
- w_out: bfloat16 [1024, 1024], P('items'), may hold values from -4 to 4
- w_up: bfloat16 [1024, 4096], P('items'), may hold values from -0.1875 to 0.1875
- w_down: bfloat16 [4096, 1024], P('items'), may hold values from -0.09375 to 0.09375
- w_ada_one: bfloat16 [1024, 2048], P('items'), may hold values from -0.09375 to 0.09375
- w_ada_two: bfloat16 [1024, 2048], P('items'), may hold values from -0.09375 to 0.09375
Outputs:
- layer_out: bfloat16 [16, 1280, 1024], P('items', 'seq')
- input_grad: float32 [16, 1280, 1024], P('items', 'seq')
- grad_query: float32 [1024, 1024], P(('items', 'seq'))
- grad_key: float32 [1024, 1024], P(('items', 'seq'))
- grad_value: float32 [1024, 1024], P(('items', 'seq'))
- grad_out: float32 [1024, 1024], P(('items', 'seq'))
- grad_up: float32 [1024, 4096], P(('items', 'seq'))
- grad_down: float32 [4096, 1024], P(('items', 'seq'))
- grad_ada_one: float32 [1024, 2048], P(('items', 'seq'))
- grad_ada_two: float32 [1024, 2048], P(('items', 'seq'))
- grad_table: float32 [8, 1024], P(None, ('items', 'seq'))
Inputs may be any that keep to these rules, and one draw needn't show every extreme that they name: `prompt_len`: prompt frames at and past an item's length are padding. `section_ids`: the number of items per section is uneven across sections.
All inputs are finite; a program needn't handle non-finite values.
Results may differ from a plain program's by a relative error of at most 0.019.
Values may be sent and summed in bfloat16 or wider, within the bound.
No kernel may reach another device: no remote copies, remote signals or barrier semaphores. Data moves between devices by JAX's collectives and lax.ppermute only.
A program may use at most 384 MiB of HBM per device.

v0:
```python
from functools import partial
import math
import jax
import jax.numpy as jnp
from jax import lax
from jax.sharding import PartitionSpec as P

HEADS = 16
HEAD_DIM = 64
PROMPT = 640
EPSILON = 1e-05
MASKED = -1e30


def exact(left, right):
    return jnp.dot(left, right, precision=lax.Precision.HIGHEST)


def dot_rows(left, right):
    return lax.dot_general(
        left, right, (((0,), (0,)), ((), ())), preferred_element_type=jnp.float32
    )


def dot_last(left, right):
    return lax.dot_general(
        left, right, (((1,), (1,)), ((), ())), preferred_element_type=jnp.float32
    )


def ada_norm(values, ada):
    width = values.shape[-1]
    centred = values - jnp.mean(values, axis=-1, keepdims=True)
    spread = jnp.mean(centred * centred, axis=-1, keepdims=True)
    normed = centred * lax.rsqrt(spread + EPSILON)
    return (1.0 + ada[:, None, :width]) * normed + ada[:, None, width:]


def split_heads(block):
    return block.reshape(block.shape[0], HEADS, HEAD_DIM)


def frames_major(grad, dim, items_count, seq_count):
    shape = grad.shape
    piece = shape[dim] // (items_count * seq_count)
    parted = grad.reshape(shape[:dim] + (items_count, seq_count, piece) + shape[dim + 1 :])
    return jnp.swapaxes(parted, dim, dim + 1).reshape(shape)


def shards(
    tokens,
    cotangent,
    prompt_len,
    section_ids,
    section_table,
    w_query,
    w_key,
    w_value,
    w_out,
    w_up,
    w_down,
    w_ada_one,
    w_ada_two,
):
    full_query, full_key, full_value, full_out, full_up, full_down, full_ada_one, full_ada_two = (
        lax.all_gather(w_query, "items", axis=0, tiled=True),
        lax.all_gather(w_key, "items", axis=0, tiled=True),
        lax.all_gather(w_value, "items", axis=0, tiled=True),
        lax.all_gather(w_out, "items", axis=0, tiled=True),
        lax.all_gather(w_up, "items", axis=0, tiled=True),
        lax.all_gather(w_down, "items", axis=0, tiled=True),
        lax.all_gather(w_ada_one, "items", axis=0, tiled=True),
        lax.all_gather(w_ada_two, "items", axis=0, tiled=True),
    )
    batch, rows, width = tokens.shape
    items_count = lax.axis_size("items")
    seq_count = lax.axis_size("seq")
    frames_all = rows * seq_count
    scale = 1.0 / math.sqrt(HEAD_DIM)
    position = lax.axis_index("seq") * rows + jnp.arange(rows)
    key_place = jnp.arange(frames_all)
    inputs = tokens.astype(jnp.float32)
    choose = (section_ids[:, None] == jnp.arange(section_table.shape[0])[None, :]).astype(
        jnp.float32
    )
    cond = exact(choose, section_table.astype(jnp.float32))
    ada_one_w = full_ada_one.astype(jnp.float32)
    ada_two_w = full_ada_two.astype(jnp.float32)
    ada_one = exact(cond, ada_one_w)
    ada_two = exact(cond, ada_two_w)
    normed_one, back_one = jax.vjp(ada_norm, inputs, ada_one)
    low_one = normed_one.astype(jnp.bfloat16).reshape(-1, width)
    query = (
        jnp.dot(low_one, full_query, preferred_element_type=jnp.float32)
        .astype(jnp.bfloat16)
        .reshape(batch, rows, width)
    )
    keys_here = (
        jnp.dot(low_one, full_key, preferred_element_type=jnp.float32)
        .astype(jnp.bfloat16)
        .reshape(batch, rows, width)
    )
    values_here = (
        jnp.dot(low_one, full_value, preferred_element_type=jnp.float32)
        .astype(jnp.bfloat16)
        .reshape(batch, rows, width)
    )
    keys_all, values_all = (
        lax.all_gather(keys_here, "seq", axis=1, tiled=True),
        lax.all_gather(values_here, "seq", axis=1, tiled=True),
    )

    def masked_scores(query_item, keys_item, length, query_place, key_spot):
        raw = (
            jnp.einsum(
                "qhd,khd->hqk",
                split_heads(query_item),
                split_heads(keys_item),
                preferred_element_type=jnp.float32,
            )
            * scale
        )
        allowed = (key_spot[None, :] < length) | (key_spot[None, :] >= PROMPT) & (
            query_place[:, None] >= PROMPT
        )
        return jnp.where(allowed[None], raw, MASKED)

    def attend(packed):
        query_item, keys_item, values_item, length = packed
        scores = masked_scores(query_item, keys_item, length, position, key_place)
        peak = jnp.max(scores, axis=-1, keepdims=True)
        expo = jnp.exp(scores - peak)
        total = jnp.sum(expo, axis=-1, keepdims=True)
        probs = (expo / total).astype(jnp.bfloat16)
        mixed_item = jnp.einsum(
            "hqk,khd->qhd", probs, split_heads(values_item), preferred_element_type=jnp.float32
        )
        return (
            mixed_item.astype(jnp.bfloat16).reshape(rows, width),
            (peak + jnp.log(total))[..., 0],
        )

    mixed, log_total = lax.map(attend, (query, keys_all, values_all, prompt_len))
    mixed_flat = mixed.reshape(-1, width)
    attended = inputs + jnp.dot(mixed_flat, full_out, preferred_element_type=jnp.float32).reshape(
        batch, rows, width
    )
    normed_two, back_two = jax.vjp(ada_norm, attended, ada_two)
    low_two = normed_two.astype(jnp.bfloat16).reshape(-1, width)
    upward = jnp.dot(low_two, full_up, preferred_element_type=jnp.float32)
    active, gelu_back = jax.vjp(partial(jax.nn.gelu, approximate=False), upward)
    active_low = active.astype(jnp.bfloat16)
    layer_out = (
        attended
        + jnp.dot(active_low, full_down, preferred_element_type=jnp.float32).reshape(
            batch, rows, width
        )
    ).astype(jnp.bfloat16)
    grad_top = cotangent.astype(jnp.float32)
    grad_low = cotangent.reshape(-1, width)
    grad_down = dot_rows(active_low, grad_low)
    (grad_upward,) = gelu_back(dot_last(grad_low, full_down))
    upward_low = grad_upward.astype(jnp.bfloat16)
    grad_up = dot_rows(low_two, upward_low)
    grad_normed_two = dot_last(upward_low, full_up).reshape(batch, rows, width)
    back_mid, grad_ada_two_rows = back_two(grad_normed_two)
    grad_attended = grad_top + back_mid
    grad_ada_two = exact(cond.T, grad_ada_two_rows)
    attended_low = grad_attended.astype(jnp.bfloat16).reshape(-1, width)
    grad_out = dot_rows(mixed_flat, attended_low)
    grad_mixed = dot_last(attended_low, full_out).astype(jnp.bfloat16).reshape(batch, rows, width)

    def score_grads(
        query_item, keys_item, values_item, length, log_item, grad_item, query_place, key_spot
    ):
        scores = masked_scores(query_item, keys_item, length, query_place, key_spot)
        probs = jnp.exp(scores - log_item[..., None])
        grad_heads = split_heads(grad_item)
        grad_probs = jnp.einsum(
            "qhd,khd->hqk", grad_heads, split_heads(values_item), preferred_element_type=jnp.float32
        )
        inner = jnp.sum(probs * grad_probs, axis=-1, keepdims=True)
        grad_scores = (probs * (grad_probs - inner)).astype(jnp.bfloat16)
        return (probs, grad_heads, grad_scores, inner[..., 0])

    def attend_back(packed):
        query_item, keys_item, values_item, length, log_item, grad_item = packed
        probs, grad_heads, grad_scores, inner = score_grads(
            query_item, keys_item, values_item, length, log_item, grad_item, position, key_place
        )
        grad_query_item = (
            jnp.einsum(
                "hqk,khd->qhd",
                grad_scores,
                split_heads(keys_item),
                preferred_element_type=jnp.float32,
            )
            * scale
        )
        grad_keys_item = (
            jnp.einsum(
                "hqk,qhd->khd",
                grad_scores,
                split_heads(query_item),
                preferred_element_type=jnp.float32,
            )
            * scale
        )
        grad_values_item = jnp.einsum(
            "hqk,qhd->khd",
            probs.astype(jnp.bfloat16),
            grad_heads,
            preferred_element_type=jnp.float32,
        )
        return (
            grad_query_item.reshape(rows, width),
            grad_keys_item.reshape(frames_all, width),
            grad_values_item.reshape(frames_all, width),
        )

    grad_query_rows, grad_keys_all, grad_values_all = lax.map(
        attend_back, (query, keys_all, values_all, prompt_len, log_total, grad_mixed)
    )
    grad_keys_here, grad_values_here = (
        lax.psum_scatter(
            grad_keys_all.astype(jnp.bfloat16), "seq", scatter_dimension=1, tiled=True
        ).astype(jnp.float32),
        lax.psum_scatter(
            grad_values_all.astype(jnp.bfloat16), "seq", scatter_dimension=1, tiled=True
        ).astype(jnp.float32),
    )
    query_low = grad_query_rows.astype(jnp.bfloat16).reshape(-1, width)
    keys_low = grad_keys_here.astype(jnp.bfloat16).reshape(-1, width)
    values_low = grad_values_here.astype(jnp.bfloat16).reshape(-1, width)
    grad_query = dot_rows(low_one, query_low)
    grad_key = dot_rows(low_one, keys_low)
    grad_value = dot_rows(low_one, values_low)
    grad_normed_one = (
        dot_last(query_low, full_query)
        + dot_last(keys_low, full_key)
        + dot_last(values_low, full_value)
    )
    back_in, grad_ada_one_rows = back_one(grad_normed_one.reshape(batch, rows, width))
    input_grad = grad_attended + back_in
    grad_ada_one = exact(cond.T, grad_ada_one_rows)
    grad_cond = exact(grad_ada_one_rows, ada_one_w.T) + exact(grad_ada_two_rows, ada_two_w.T)
    grad_table = exact(choose.T, grad_cond)
    table_t = frames_major(grad_table, 1, items_count, seq_count)
    part_query = frames_major(grad_query, 0, items_count, seq_count)
    part_key = frames_major(grad_key, 0, items_count, seq_count)
    part_value = frames_major(grad_value, 0, items_count, seq_count)
    part_out = frames_major(grad_out, 0, items_count, seq_count)
    part_ada_one = frames_major(grad_ada_one, 0, items_count, seq_count)
    part_up = frames_major(grad_up, 0, items_count, seq_count)
    part_down = frames_major(grad_down, 0, items_count, seq_count)
    part_ada_two = frames_major(grad_ada_two, 0, items_count, seq_count)
    (
        seq_query,
        seq_key,
        seq_value,
        seq_out,
        seq_up,
        seq_down,
        seq_ada_one,
        seq_ada_two,
        seq_table,
    ) = (
        lax.psum_scatter(
            part_query.astype(jnp.bfloat16), "seq", scatter_dimension=0, tiled=True
        ).astype(jnp.float32),
        lax.psum_scatter(
            part_key.astype(jnp.bfloat16), "seq", scatter_dimension=0, tiled=True
        ).astype(jnp.float32),
        lax.psum_scatter(
            part_value.astype(jnp.bfloat16), "seq", scatter_dimension=0, tiled=True
        ).astype(jnp.float32),
        lax.psum_scatter(
            part_out.astype(jnp.bfloat16), "seq", scatter_dimension=0, tiled=True
        ).astype(jnp.float32),
        lax.psum_scatter(
            part_up.astype(jnp.bfloat16), "seq", scatter_dimension=0, tiled=True
        ).astype(jnp.float32),
        lax.psum_scatter(
            part_down.astype(jnp.bfloat16), "seq", scatter_dimension=0, tiled=True
        ).astype(jnp.float32),
        lax.psum_scatter(
            part_ada_one.astype(jnp.bfloat16), "seq", scatter_dimension=0, tiled=True
        ).astype(jnp.float32),
        lax.psum_scatter(
            part_ada_two.astype(jnp.bfloat16), "seq", scatter_dimension=0, tiled=True
        ).astype(jnp.float32),
        lax.psum_scatter(
            table_t.astype(jnp.bfloat16), "seq", scatter_dimension=1, tiled=True
        ).astype(jnp.float32),
    )
    (
        grad_query,
        grad_key,
        grad_value,
        grad_out,
        grad_up,
        grad_down,
        grad_ada_one,
        grad_ada_two,
        grad_table,
    ) = (
        lax.psum_scatter(
            seq_query.astype(jnp.bfloat16), "items", scatter_dimension=0, tiled=True
        ).astype(jnp.float32),
        lax.psum_scatter(
            seq_key.astype(jnp.bfloat16), "items", scatter_dimension=0, tiled=True
        ).astype(jnp.float32),
        lax.psum_scatter(
            seq_value.astype(jnp.bfloat16), "items", scatter_dimension=0, tiled=True
        ).astype(jnp.float32),
        lax.psum_scatter(
            seq_out.astype(jnp.bfloat16), "items", scatter_dimension=0, tiled=True
        ).astype(jnp.float32),
        lax.psum_scatter(
            seq_up.astype(jnp.bfloat16), "items", scatter_dimension=0, tiled=True
        ).astype(jnp.float32),
        lax.psum_scatter(
            seq_down.astype(jnp.bfloat16), "items", scatter_dimension=0, tiled=True
        ).astype(jnp.float32),
        lax.psum_scatter(
            seq_ada_one.astype(jnp.bfloat16), "items", scatter_dimension=0, tiled=True
        ).astype(jnp.float32),
        lax.psum_scatter(
            seq_ada_two.astype(jnp.bfloat16), "items", scatter_dimension=0, tiled=True
        ).astype(jnp.float32),
        lax.psum_scatter(
            seq_table.astype(jnp.bfloat16), "items", scatter_dimension=1, tiled=True
        ).astype(jnp.float32),
    )
    return (
        layer_out,
        input_grad,
        grad_query,
        grad_key,
        grad_value,
        grad_out,
        grad_up,
        grad_down,
        grad_ada_one,
        grad_ada_two,
        grad_table,
    )


def solution(mesh):
    return jax.shard_map(
        shards,
        mesh=mesh,
        in_specs=(
            P("items", "seq", None),
            P("items", "seq", None),
            P("items"),
            P("items"),
            P(),
            P("items", None),
            P("items", None),
            P("items", None),
            P("items", None),
            P("items", None),
            P("items", None),
            P("items", None),
            P("items", None),
        ),
        out_specs=(
            P("items", "seq", None),
            P("items", "seq", None),
            P(("items", "seq"), None),
            P(("items", "seq"), None),
            P(("items", "seq"), None),
            P(("items", "seq"), None),
            P(("items", "seq"), None),
            P(("items", "seq"), None),
            P(("items", "seq"), None),
            P(("items", "seq"), None),
            P(None, ("items", "seq")),
        ),
        check_vma=False,
    )
```

profile of v0, /device:TPU:0, one launch (start us, length us, event | category | flops | bytes accessed | tf_op | source)
XLA Modules:
  0.0 1794.8 jit_solution(3981334618277993144)
XLA Ops:
  14.1 49.4 %all-gather.13.cloned.1.call-done = bf16[1024,2048]{1,0:T(8,128)(2,1)} async-done(((bf16[64,2048]{1,0:T(8,128)(2,1)}), bf16[1024,2048]{1,0:T(8,128)(2,1)}) %all-gather.13.cloned.1.call-update) | async-done | bytes 4194320 | tf_op jit(solution)/shard_map/all_gather | solution.py:72
  67.4 38.1 %all-gather.19.cloned.1.call-done = bf16[1024,1024]{1,0:T(8,128)(2,1)} async-done(((bf16[64,1024]{1,0:T(8,128)(2,1)}), bf16[1024,1024]{1,0:T(8,128)(2,1)}) %all-gather.19.cloned.1.call-update) | async-done | bytes 2097168 | tf_op jit(solution)/shard_map/all_gather | solution.py:67
  109.9 38.1 %all-gather.15.cloned.1.call-done = bf16[1024,1024]{1,0:T(8,128)(2,1)} async-done(((bf16[64,1024]{1,0:T(8,128)(2,1)}), bf16[1024,1024]{1,0:T(8,128)(2,1)}) %all-gather.15.cloned.1.call-update) | async-done | bytes 2097168 | tf_op jit(solution)/shard_map/all_gather | solution.py:68
  155.7 43.8 %all-gather.23.cloned.1.call-done = bf16[1024,2048]{1,0:T(8,128)(2,1)} async-done(((bf16[64,2048]{1,0:T(8,128)(2,1)}), bf16[1024,2048]{1,0:T(8,128)(2,1)}) %all-gather.23.cloned.1.call-update) | async-done | bytes 4194320 | tf_op jit(solution)/shard_map/all_gather | solution.py:73
  203.4 38.0 %all-gather.17.cloned.1.call-done = bf16[1024,1024]{1,0:T(8,128)(2,1)} async-done(((bf16[64,1024]{1,0:T(8,128)(2,1)}), bf16[1024,1024]{1,0:T(8,128)(2,1)}) %all-gather.17.cloned.1.call-update) | async-done | bytes 2097168 | tf_op jit(solution)/shard_map/all_gather | solution.py:66
  246.1 35.2 %all-gather.31.cloned.1.call-done = bf16[1280,1024]{1,0:T(8,128)(2,1)} async-done(((bf16[640,1024]{1,0:T(8,128)(2,1)}), bf16[1280,1024]{1,0:T(8,128)(2,1)}) %all-gather.31.cloned.1.call-update) | async-done | bytes 2621456 | tf_op jit(solution)/shard_map/all_gather | solution.py:109
  284.3 23.1 %fusion.93 = (f32[16,640]{1,0:T(8,128)S(1)}, f32[16,640,1280]{2,1,0:T(8,128)}) fusion(bf16[640,16,64]{0,2,1:T(8,128)(2,1)} %bitcast.284, bf16[1280,16,64]{0,2,1:T(8,128)(2,1)S(1)} %bitcast.278, pred[640,1280]{1,0:T(8,128)(4,1)S(1)} %and_or_fusion), kind=kOutput, calls=%fused_computation.153 | convolution fusion | flops 1717032960 | bytes 57221120 | tf_op jit(solution)/shard_map/while/body/eval_jaxpr/qhd,khd->hqk/dot_general | solution.py:115
  307.4 16.8 fusion
  328.6 20.2 %fusion.50 = bf16[16,64,640]{2,1,0:T(8,128)(2,1)S(1)} fusion(bf16[1280,16,64]{0,2,1:T(8,128)(2,1)} %bitcast.289, f32[16,640,1280]{2,1,0:T(8,128)} %get-tuple-element.90, f32[16,640]{1,0:T(8,128)S(1)} %fusion, f32[16,640]{1,0:T(8,128)S(1)} %get-tuple-element.89), kind=kOutput, calls=%fused_computation.97 | convolution fusion | flops 1717698560 | bytes 56442880 | tf_op jit(solution)/shard_map/while/body/eval_jaxpr/hqk,khd->qhd/dot_general | solution.py:135
  348.8 17.3 all-gather.21.cloned.1.call-done
  371.3 70.7 %all-gather.25.cloned.1.call-done = bf16[1024,4096]{1,0:T(8,128)(2,1)} async-done(((bf16[64,4096]{1,0:T(8,128)(2,1)}), bf16[1024,4096]{1,0:T(8,128)(2,1)}) %all-gather.25.cloned.1.call-update) | async-done | bytes 8388624 | tf_op jit(solution)/shard_map/all_gather | solution.py:70
  442.0 32.4 %fusion.6 = (f32[640,4096]{1,0:T(8,128)}, f32[640,4096]{1,0:T(8,128)}) fusion(bf16[1024,4096]{1,0:T(8,128)(2,1)} %all-gather.25.cloned.1.call-done, f32[1024]{0:T(1024)S(1)} %bitcast.330, f32[640]{0:T(1024)S(1)} %fusion.78, f32[1,640,1024]{2,1,0:T(8,128)} %copy-done.6, f32[640]{0:T(1024)S(1)} %broadcast_multiply_fusion, f32[1024]{0:T(1024)S(1)} %bitcast.310), kind=kOutput, calls=%fused_computation.13 | convolution fusion | flops 5534515200 | bytes 31994880 | tf_op jit(solution)/shard_map/dot_general | solution.py:150
  474.4 42.8 %all-gather.27.cloned.1.call-done = bf16[4096,1024]{1,0:T(8,128)(2,1)} async-done(((bf16[256,1024]{1,0:T(8,128)(2,1)}), bf16[4096,1024]{1,0:T(8,128)(2,1)}) %all-gather.27.cloned.1.call-update) | async-done | bytes 8388624 | tf_op jit(solution)/shard_map/all_gather | solution.py:71
  552.4 38.6 %multiply_reduce_fusion = (f32[16,640]{1,0:T(8,128)S(1)}, f32[16,640,1280]{2,1,0:T(8,128)}) fusion(f32[16,640,1280]{2,1,0:T(8,128)} %get-tuple-element.90, f32[16,640]{1,0:T(8,128)S(1)} %log_add_fusion, bf16[640,16,64]{0,2,1:T(8,128)(2,1)S(1)} %bitcast.287, bf16[1280,16,64]{0,2,1:T(8,128)(2,1)} %bitcast.290), kind=kOutput, calls=%fused_computation.1 | convolution fusion | flops 1717032960 | bytes 108871680 | tf_op jit(solution)/shard_map/while/body/eval_jaxpr/qhd,khd->hqk/dot_general | solution.py:179
  591.0 42.2 %multiply_convert_fusion = bf16[16,640,1280]{2,1,0:T(8,128)(2,1)} fusion(f32[16,640,1280]{2,1,0:T(8,128)} %get-tuple-element.96, f32[16,640,1280]{2,1,0:T(8,128)} %get-tuple-element.90, f32[16,640]{1,0:T(8,128)S(1)} %get-tuple-element.95, f32[16,640]{1,0:T(8,128)S(1)} %log_add_fusion), kind=kLoop, calls=%fused_computation | loop fusion | flops 52428800 | bytes 131153920 | tf_op jit(solution)/shard_map/while/body/eval_jaxpr/convert_element_type | solution.py:183
  652.4 21.5 %fusion.36 = bf16[16,64,1280]{2,1,0:T(8,128)(2,1)} fusion(bf16[640,16,64]{0,2,1:T(8,128)(2,1)S(1)} %bitcast.288, f32[16,640,1280]{2,1,0:T(8,128)} %get-tuple-element.90, f32[16,640]{1,0:T(8,128)S(1)} %log_add_fusion), kind=kOutput, calls=%fused_computation.67 | convolution fusion | flops 1705246720 | bytes 56401920 | tf_op jit(solution)/shard_map/while/body/eval_jaxpr/hqk,qhd->khd/dot_general | solution.py:209
  708.7 19.5 %reduce-scatter.25.cloned.1.call-done = bf16[1,640,1024]{2,1,0:T(8,128)(2,1)} async-done(((bf16[1,1280,1024]{2,1,0:T(8,128)(2,1)}), bf16[1,640,1024]{2,1,0:T(8,128)(2,1)}) %reduce-scatter.25.cloned.1.call-update) | async-done | bytes 1310736 | tf_op jit(solution)/shard_map/reduce_scatter | solution.py:228
  794.7 24.6 %fusion.9 = bf16[4096,640]{0,1:T(8,128)(2,1)} fusion(f32[640,4096]{1,0:T(8,128)} %get-tuple-element.94), kind=kLoop, calls=%fused_computation.16 | loop fusion | flops 170393600 | bytes 15728640 | tf_op jit(solution)/shard_map/convert_element_type | solution.py:152
  855.6 34.0 %reduce-scatter.31.cloned.1.call-done = bf16[512,1024]{1,0:T(8,128)(2,1)} async-done(((bf16[1024,1024]{1,0:T(8,128)(2,1)}), bf16[512,1024]{1,0:T(8,128)(2,1)}) %reduce-scatter.31.cloned.1.call-update) | async-done | bytes 1048592 | tf_op jit(solution)/shard_map/reduce_scatter | solution.py:271
  889.7 56.4 %reduce-scatter.55.cloned.1.call-done = bf16[512,2048]{1,0:T(8,128)(2,1)} async-done(((bf16[1024,2048]{1,0:T(8,128)(2,1)}), bf16[512,2048]{1,0:T(8,128)(2,1)}) %reduce-scatter.55.cloned.1.call-update) | async-done | bytes 2097168 | tf_op jit(solution)/shard_map/reduce_scatter | solution.py:289
  946.2 56.7 %reduce-scatter.51.cloned.1.call-done = bf16[512,2048]{1,0:T(8,128)(2,1)} async-done(((bf16[1024,2048]{1,0:T(8,128)(2,1)}), bf16[512,2048]{1,0:T(8,128)(2,1)}) %reduce-scatter.51.cloned.1.call-update) | async-done | bytes 2097168 | tf_op jit(solution)/shard_map/reduce_scatter | solution.py:286
  1002.9 101.3 %reduce-scatter.43.cloned.1.call-done = bf16[512,4096]{1,0:T(8,128)(2,1)} async-done(((bf16[1024,4096]{1,0:T(8,128)(2,1)}), bf16[512,4096]{1,0:T(8,128)(2,1)}) %reduce-scatter.43.cloned.1.call-update) | async-done | bytes 4194320 | tf_op jit(solution)/shard_map/reduce_scatter | solution.py:280
  1104.5 101.4 %reduce-scatter.47.cloned.1.call-done = bf16[2048,1024]{1,0:T(8,128)(2,1)} async-done(((bf16[4096,1024]{1,0:T(8,128)(2,1)}), bf16[2048,1024]{1,0:T(8,128)(2,1)}) %reduce-scatter.47.cloned.1.call-update) | async-done | bytes 4194320 | tf_op jit(solution)/shard_map/reduce_scatter | solution.py:283
  1219.1 45.9 %reduce-scatter.61.cloned.1.call-done = bf16[32,8]{1,0:T(8,128)(2,1)} async-done(((bf16[512,8]{1,0:T(8,128)(2,1)}), bf16[32,8]{1,0:T(8,128)(2,1)}) %reduce-scatter.61.cloned.1.call-update) | async-done | bytes 528
  1266.4 58.7 %reduce-scatter.41.cloned.1.call-done = bf16[32,1024]{1,0:T(8,128)(2,1)} async-done(((bf16[512,1024]{1,0:T(8,128)(2,1)}), bf16[32,1024]{1,0:T(8,128)(2,1)}) %reduce-scatter.41.cloned.1.call-update) | async-done | bytes 65552 | tf_op jit(solution)/shard_map/reduce_scatter | solution.py:316
  1326.6 58.9 %reduce-scatter.37.cloned.1.call-done = bf16[32,1024]{1,0:T(8,128)(2,1)} async-done(((bf16[512,1024]{1,0:T(8,128)(2,1)}), bf16[32,1024]{1,0:T(8,128)(2,1)}) %reduce-scatter.37.cloned.1.call-update) | async-done | bytes 65552 | tf_op jit(solution)/shard_map/reduce_scatter | solution.py:313
  1387.1 58.5 %reduce-scatter.29.cloned.1.call-done = bf16[32,1024]{1,0:T(8,128)(2,1)} async-done(((bf16[512,1024]{1,0:T(8,128)(2,1)}), bf16[32,1024]{1,0:T(8,128)(2,1)}) %reduce-scatter.29.cloned.1.call-update) | async-done | bytes 65552 | tf_op jit(solution)/shard_map/reduce_scatter | solution.py:307
  1447.0 58.9 %reduce-scatter.33.cloned.1.call-done = bf16[32,1024]{1,0:T(8,128)(2,1)} async-done(((bf16[512,1024]{1,0:T(8,128)(2,1)}), bf16[32,1024]{1,0:T(8,128)(2,1)}) %reduce-scatter.33.cloned.1.call-update) | async-done | bytes 65552 | tf_op jit(solution)/shard_map/reduce_scatter | solution.py:310
  1507.4 62.7 %reduce-scatter.57.cloned.1.call-done = bf16[32,2048]{1,0:T(8,128)(2,1)} async-done(((bf16[512,2048]{1,0:T(8,128)(2,1)}), bf16[32,2048]{1,0:T(8,128)(2,1)}) %reduce-scatter.57.cloned.1.call-update) | async-done | bytes 131088 | tf_op jit(solution)/shard_map/reduce_scatter | solution.py:328
  1571.8 63.1 %reduce-scatter.53.cloned.1.call-done = bf16[32,2048]{1,0:T(8,128)(2,1)} async-done(((bf16[512,2048]{1,0:T(8,128)(2,1)}), bf16[32,2048]{1,0:T(8,128)(2,1)}) %reduce-scatter.53.cloned.1.call-update) | async-done | bytes 131088 | tf_op jit(solution)/shard_map/reduce_scatter | solution.py:325
  1636.5 73.8 %reduce-scatter.45.cloned.1.call-done = bf16[32,4096]{1,0:T(8,128)(2,1)} async-done(((bf16[512,4096]{1,0:T(8,128)(2,1)}), bf16[32,4096]{1,0:T(8,128)(2,1)}) %reduce-scatter.45.cloned.1.call-update) | async-done | bytes 262160 | tf_op jit(solution)/shard_map/reduce_scatter | solution.py:319
  1712.1 73.8 %reduce-scatter.49.cloned.1.call-done = bf16[128,1024]{1,0:T(8,128)(2,1)} async-done(((bf16[2048,1024]{1,0:T(8,128)(2,1)}), bf16[128,1024]{1,0:T(8,128)(2,1)}) %reduce-scatter.49.cloned.1.call-update) | async-done | bytes 262160 | tf_op jit(solution)/shard_map/reduce_scatter | solution.py:322
  (216 shorter events, 261.7 us)
Async XLA Ops:
  7.2 56.3 %all-gather.13.cloned.1.call-start = ((), (), s32[]{:S(2)}) async-start(), calls=%async_computation.20 | async-start | bytes 4456448 | tf_op jit(solution)/shard_map/all_gather | solution.py:72
  7.9 97.6 %all-gather.19.cloned.1.call-start = ((), (), s32[]{:S(2)}) async-start(), calls=%async_computation.23 | async-start | bytes 2228224 | tf_op jit(solution)/shard_map/all_gather | solution.py:67
  8.7 139.3 %all-gather.15.cloned.1.call-start = ((), (), s32[]{:S(2)}) async-start(), calls=%async_computation.21 | async-start | bytes 2228224 | tf_op jit(solution)/shard_map/all_gather | solution.py:68
  9.4 190.1 %all-gather.23.cloned.1.call-start = ((), (), s32[]{:S(2)}) async-start(), calls=%async_computation.25 | async-start | bytes 4456448 | tf_op jit(solution)/shard_map/all_gather | solution.py:73
  10.0 231.5 %all-gather.17.cloned.1.call-start = ((), (), s32[]{:S(2)}) async-start(), calls=%async_computation.22 | async-start | bytes 2228224 | tf_op jit(solution)/shard_map/all_gather | solution.py:66
  10.6 270.7 %all-gather.31.cloned.1.call-start = ((), (), s32[]{:S(2)}) async-start(), calls=%async_computation.48 | async-start | bytes 3932160 | tf_op jit(solution)/shard_map/all_gather | solution.py:109
  12.9 228.6 %copy-start.17 = (f32[640]{0:T(1024)}, f32[640]{0:T(1024)S(1)}, u32[]{:S(2)}) copy-start(f32[640]{0:T(1024)S(1)} %broadcast_multiply_fusion.1) | copy-start | bytes 7684
  109.8 214.4 %all-gather.29.cloned.1.call-start = ((), (), s32[]{:S(2)}) async-start(), calls=%async_computation.47 | async-start | bytes 3932160 | tf_op jit(solution)/shard_map/all_gather | solution.py:110
  152.2 213.9 %all-gather.21.cloned.1.call-start = ((), (), s32[]{:S(2)}) async-start(), calls=%async_computation.24 | async-start | bytes 2228224 | tf_op jit(solution)/shard_map/all_gather | solution.py:69
  153.0 289.0 %all-gather.25.cloned.1.call-start = ((), (), s32[]{:S(2)}) async-start(), calls=%async_computation.26 | async-start | bytes 8912896 | tf_op jit(solution)/shard_map/all_gather | solution.py:70
  153.7 363.5 %all-gather.27.cloned.1.call-start = ((), (), s32[]{:S(2)}) async-start(), calls=%async_computation.27 | async-start | bytes 8912896 | tf_op jit(solution)/shard_map/all_gather | solution.py:71
  154.3 550.0 %reduce-scatter.23.cloned.1.call-start = ((), (), s32[]{:S(2)}) async-start(), calls=%async_computation.28 | async-start | bytes 3932160 | tf_op jit(solution)/shard_map/reduce_scatter | solution.py:225
  652.4 75.8 %reduce-scatter.25.cloned.1.call-start = ((), (), s32[]{:S(2)}) async-start(), calls=%async_computation.29 | async-start | bytes 3932160 | tf_op jit(solution)/shard_map/reduce_scatter | solution.py:228
  678.4 168.8 %reduce-scatter.59.cloned.1.call-start = ((), (), s32[]{:S(2)}) async-start(), calls=%async_computation.46 | async-start | bytes 24576 | tf_op jit(solution)/shard_map/reduce_scatter | solution.py:292
  743.7 105.1 %reduce-scatter.39.cloned.1.call-start = ((), (), s32[]{:S(2)}) async-start(), calls=%async_computation.36 | async-start | bytes 3145728 | tf_op jit(solution)/shard_map/reduce_scatter | solution.py:277
  749.2 100.3 %reduce-scatter.35.cloned.1.call-start = ((), (), s32[]{:S(2)}) async-start(), calls=%async_computation.34 | async-start | bytes 3145728 | tf_op jit(solution)/shard_map/reduce_scatter | solution.py:274
  758.9 96.6 %reduce-scatter.27.cloned.1.call-start = ((), (), s32[]{:S(2)}) async-start(), calls=%async_computation.30 | async-start | bytes 3145728 | tf_op jit(solution)/shard_map/reduce_scatter | solution.py:268
  762.6 127.0 %reduce-scatter.31.cloned.1.call-start = ((), (), s32[]{:S(2)}) async-start(), calls=%async_computation.32 | async-start | bytes 3145728 | tf_op jit(solution)/shard_map/reduce_scatter | solution.py:271
  766.7 179.4 %reduce-scatter.55.cloned.1.call-start = ((), (), s32[]{:S(2)}) async-start(), calls=%async_computation.44 | async-start | bytes 6291456 | tf_op jit(solution)/shard_map/reduce_scatter | solution.py:289
  773.3 229.5 %reduce-scatter.51.cloned.1.call-start = ((), (), s32[]{:S(2)}) async-start(), calls=%async_computation.42 | async-start | bytes 6291456 | tf_op jit(solution)/shard_map/reduce_scatter | solution.py:286
  774.1 330.2 %reduce-scatter.43.cloned.1.call-start = ((), (), s32[]{:S(2)}) async-start(), calls=%async_computation.38 | async-start | bytes 12582912 | tf_op jit(solution)/shard_map/reduce_scatter | solution.py:280
  794.7 411.2 %reduce-scatter.47.cloned.1.call-start = ((), (), s32[]{:S(2)}) async-start(), calls=%async_computation.40 | async-start | bytes 12582912 | tf_op jit(solution)/shard_map/reduce_scatter | solution.py:283
  847.1 417.9 %reduce-scatter.61.cloned.1.call-start = ((), (), s32[]{:S(2)}) async-start(), calls=%async_computation.49 | async-start | bytes 139264
  848.7 476.4 %reduce-scatter.41.cloned.1.call-start = ((), (), s32[]{:S(2)}) async-start(), calls=%async_computation.37 | async-start | bytes 1114112 | tf_op jit(solution)/shard_map/reduce_scatter | solution.py:316
  849.5 536.1 %reduce-scatter.37.cloned.1.call-start = ((), (), s32[]{:S(2)}) async-start(), calls=%async_computation.35 | async-start | bytes 1114112 | tf_op jit(solution)/shard_map/reduce_scatter | solution.py:313
  850.0 595.5 %reduce-scatter.29.cloned.1.call-start = ((), (), s32[]{:S(2)}) async-start(), calls=%async_computation.31 | async-start | bytes 1114112 | tf_op jit(solution)/shard_map/reduce_scatter | solution.py:307
  855.6 650.3 %reduce-scatter.33.cloned.1.call-start = ((), (), s32[]{:S(2)}) async-start(), calls=%async_computation.33 | async-start | bytes 1114112 | tf_op jit(solution)/shard_map/reduce_scatter | solution.py:310
  889.6 680.5 %reduce-scatter.57.cloned.1.call-start = ((), (), s32[]{:S(2)}) async-start(), calls=%async_computation.45 | async-start | bytes 2228224 | tf_op jit(solution)/shard_map/reduce_scatter | solution.py:328
  946.1 688.8 %reduce-scatter.53.cloned.1.call-start = ((), (), s32[]{:S(2)}) async-start(), calls=%async_computation.43 | async-start | bytes 2228224 | tf_op jit(solution)/shard_map/reduce_scatter | solution.py:325
  1002.9 707.5 %reduce-scatter.45.cloned.1.call-start = ((), (), s32[]{:S(2)}) async-start(), calls=%async_computation.39 | async-start | bytes 4456448 | tf_op jit(solution)/shard_map/reduce_scatter | solution.py:319
  1104.3 681.6 %reduce-scatter.49.cloned.1.call-start = ((), (), s32[]{:S(2)}) async-start(), calls=%async_computation.41 | async-start | bytes 4456448 | tf_op jit(solution)/shard_map/reduce_scatter | solution.py:322
  1206.0 581.7 %copy-start.1 = (bf16[8,1024]{1,0:T(8,128)(2,1)S(1)}, bf16[8,1024]{1,0:T(8,128)(2,1)}, u32[]{:S(2)}) copy-start(bf16[8,1024]{1,0:T(8,128)(2,1)} %param.17) | copy-start | bytes 49156
  (31 other events, 1194.7 us)
Sparse Core Ops, SparseCore 0:
  10.2 53.2 all-gather.12
  65.7 39.8 all-gather.18
  107.7 40.1 all-gather.14
  150.0 49.4 all-gather.22
  201.5 39.9 all-gather.16
  243.4 37.7 all-gather.30
  283.4 39.0 all-gather.28
  324.6 41.4 all-gather.20
  368.3 73.6 all-gather.24
  444.0 73.1 all-gather.26
  652.5 35.8 reduce-scatter.22
  690.5 37.5 reduce-scatter.24
  743.8 9.7 reduce-scatter.58
  755.7 31.8 reduce-scatter.38
  789.7 31.8 reduce-scatter.34
  823.7 31.8 reduce-scatter.26
  857.7 31.8 reduce-scatter.30
  891.8 54.2 reduce-scatter.54
  948.5 54.3 reduce-scatter.50
  1005.0 99.2 reduce-scatter.42
  1106.7 99.2 reduce-scatter.46
  1210.0 55.0 reduce-scatter.60
  1268.7 56.3 reduce-scatter.40
  1329.0 56.4 reduce-scatter.36
  1389.2 56.3 reduce-scatter.28
  1449.5 56.4 reduce-scatter.32
  1509.5 60.5 reduce-scatter.56
  1574.3 60.5 reduce-scatter.52
  1638.8 71.5 reduce-scatter.44
  1714.5 71.3 reduce-scatter.48
where the time goes:
time: 1800 us; the launch traced here: 1790 us
  waiting for transfers between devices  1310 us (73%)
  matrix products  288 us (16%)
  other arithmetic  117 us (6%)
  local copies, waits for them, and re-layouts  60.6 us (3%)
    reduce_scatter x1, waiting for transfers between devices, shards(): lax.psum_scatter(part_down.astype(jnp.bfloat16), 'seq', scatter_dimension...  101 us
    reduce_scatter x1, waiting for transfers between devices, shards(): lax.psum_scatter(part_up.astype(jnp.bfloat16), 'seq', scatter_dimension=0...  101 us
    reduce_scatter x1, waiting for transfers between devices, shards(): lax.psum_scatter(seq_up.astype(jnp.bfloat16), 'items', scatter_dimension=...  73.8 us
    reduce_scatter x1, waiting for transfers between devices, shards(): lax.psum_scatter(seq_down.astype(jnp.bfloat16), 'items', scatter_dimensio...  73.8 us
    all_gather x1, waiting for transfers between devices, shards(): lax.all_gather(w_up, 'items', axis=0, tiled=True)  70.7 us
    reduce_scatter x1, waiting for transfers between devices, shards(): lax.psum_scatter(seq_ada_one.astype(jnp.bfloat16), 'items', scatter_dimen...  63.1 us
    reduce_scatter x1, waiting for transfers between devices, shards(): lax.psum_scatter(seq_ada_two.astype(jnp.bfloat16), 'items', scatter_dimen...  62.7 us
    reduce_scatter x1, waiting for transfers between devices, shards(): lax.psum_scatter(seq_value.astype(jnp.bfloat16), 'items', scatter_dimensi...  58.9 us
  transfers between devices with their start and end apart: 30, of which 25 were waited for; matrix products, arithmetic and copies ran while one was open for 17% of the time, Pallas kernels for 0%

commit v1 on v0

--- a/solution.py
+++ b/solution.py
@@ -10,6 +10,18 @@
 PROMPT = 640
 EPSILON = 1e-05
 MASKED = -1e30
+
+
+def gather_by_bits(x, axis, dim):
+    ways, here, step = (lax.axis_size(axis), lax.axis_index(axis), x.shape[dim])
+    line, have = (x, 1)
+    while have < ways:
+        line = jnp.concatenate(
+            [line, lax.ppermute(line, axis, [(d, (d - have) % ways) for d in range(ways)])],
+            axis=dim,
+        )
+        have = 2 * have
+    return jnp.roll(line, here * step, axis=dim)
 
 
 def exact(left, right):
@@ -70,7 +82,7 @@
         lax.all_gather(w_up, "items", axis=0, tiled=True),
         lax.all_gather(w_down, "items", axis=0, tiled=True),
         lax.all_gather(w_ada_one, "items", axis=0, tiled=True),
-        lax.all_gather(w_ada_two, "items", axis=0, tiled=True),
+        gather_by_bits(w_ada_two, "items", 0),
     )
     batch, rows, width = tokens.shape
     items_count = lax.axis_size("items")

time: 1800 us -> 1770 us (0.983)
  waiting for transfers between devices: 1310 us -> 1260 us
    ppermute x0 -> x4, waiting for transfers between devices: none -> 143 us  [gather_by_bits(): lax.ppermute(line, axis, [(d, (d - have) % ways) for d in range(ways)])]
    all_gather x1, waiting for transfers between devices: 70.7 us -> 19 us  [shards(): lax.all_gather(w_up, 'items', axis=0, tiled=True)]
    all_gather x1 -> x0, waiting for transfers between devices: 43.8 us -> none  [shards(): lax.all_gather(w_ada_two, 'items', axis=0, tiled=True)]
    all_gather x1, waiting for transfers between devices: 38 us -> 0.01 us  [shards(): lax.all_gather(w_query, 'items', axis=0, tiled=True)]
    all_gather x1, waiting for transfers between devices: 35.2 us -> 0.01 us  [shards(): lax.all_gather(keys_here, 'seq', axis=1, tiled=True)]
    unnamed x31 -> x30, waiting for transfers between devices: 53.1 us -> 52.1 us
  transfers between devices with their start and end apart: 30 -> 33, of which waited for: 25 -> 25; matrix products, arithmetic and copies ran while one was open for 17% -> 18% of each run, Pallas kernels for 0% -> 0%
where the time goes in v1:
time: 1770 us; the launch traced here: 1760 us
  waiting for transfers between devices  1260 us (71%)
  matrix products  289 us (16%)
  other arithmetic  121 us (7%)
  local copies, waits for them, and re-layouts  69 us (4%)
    ppermute x4, waiting for transfers between devices, gather_by_bits(): lax.ppermute(line, axis, [(d, (d - have) % ways) for d in range(ways)])  143 us
    reduce_scatter x1, waiting for transfers between devices, shards(): lax.psum_scatter(part_up.astype(jnp.bfloat16), 'seq', scatter_dimension=0...  101 us
    reduce_scatter x1, waiting for transfers between devices, shards(): lax.psum_scatter(part_down.astype(jnp.bfloat16), 'seq', scatter_dimension...  101 us
    reduce_scatter x1, waiting for transfers between devices, shards(): lax.psum_scatter(seq_down.astype(jnp.bfloat16), 'items', scatter_dimensio...  74 us
    reduce_scatter x1, waiting for transfers between devices, shards(): lax.psum_scatter(seq_up.astype(jnp.bfloat16), 'items', scatter_dimension=...  73.9 us
    reduce_scatter x1, waiting for transfers between devices, shards(): lax.psum_scatter(seq_ada_one.astype(jnp.bfloat16), 'items', scatter_dimen...  63 us
    reduce_scatter x1, waiting for transfers between devices, shards(): lax.psum_scatter(seq_ada_two.astype(jnp.bfloat16), 'items', scatter_dimen...  62.7 us
    reduce_scatter x1, waiting for transfers between devices, shards(): lax.psum_scatter(seq_value.astype(jnp.bfloat16), 'items', scatter_dimensi...  59 us
  transfers between devices with their start and end apart: 33, of which 25 were waited for; matrix products, arithmetic and copies ran while one was open for 18% of the time, Pallas kernels for 0%

profile of v1, /device:TPU:0, one launch (start us, length us, event | category | flops | bytes accessed | tf_op | source)
XLA Modules:
  0.0 1763.7 jit_solution(14501842766483960624)
XLA Ops:
  14.2 49.3 %all-gather.12.cloned.1.call-done = bf16[1024,2048]{1,0:T(8,128)(2,1)} async-done(((bf16[64,2048]{1,0:T(8,128)(2,1)}), bf16[1024,2048]{1,0:T(8,128)(2,1)}) %all-gather.12.cloned.1.call-update) | async-done | bytes 4194320 | tf_op jit(solution)/shard_map/all_gather | solution.py:84
  67.4 38.1 %all-gather.18.cloned.1.call-done = bf16[1024,1024]{1,0:T(8,128)(2,1)} async-done(((bf16[64,1024]{1,0:T(8,128)(2,1)}), bf16[1024,1024]{1,0:T(8,128)(2,1)}) %all-gather.18.cloned.1.call-update) | async-done | bytes 2097168 | tf_op jit(solution)/shard_map/all_gather | solution.py:79
  109.9 38.0 %all-gather.14.cloned.1.call-done = bf16[1024,1024]{1,0:T(8,128)(2,1)} async-done(((bf16[64,1024]{1,0:T(8,128)(2,1)}), bf16[1024,1024]{1,0:T(8,128)(2,1)}) %all-gather.14.cloned.1.call-update) | async-done | bytes 2097168 | tf_op jit(solution)/shard_map/all_gather | solution.py:80
  175.7 33.8 %collective-permute-done.2 = bf16[256,2048]{1,0:T(8,128)(2,1)S(1)} collective-permute-done((bf16[256,2048]{1,0:T(8,128)(2,1)S(1)}, bf16[256,2048]{1,0:T(8,128)(2,1)S(1)}, u32[]{:S(2)}, u32[]{:S(2)}) %collective-permute-start.2) | collective-permute-done | bytes 1048608 | tf_op jit(solution)/shard_map/ppermute | solution.py:20
  215.1 89.1 %collective-permute-done.3 = bf16[512,2048]{1,0:T(8,128)(2,1)} collective-permute-done((bf16[512,2048]{1,0:T(8,128)(2,1)}, bf16[512,2048]{1,0:T(8,128)(2,1)}, u32[]{:S(2)}, u32[]{:S(2)}) %collective-permute-start.3) | collective-permute-done | bytes 2097184 | tf_op jit(solution)/shard_map/ppermute | solution.py:20
  321.0 22.7 %fusion.97 = (f32[16,640]{1,0:T(8,128)S(1)}, f32[16,640,1280]{2,1,0:T(8,128)}) fusion(bf16[640,16,64]{0,2,1:T(8,128)(2,1)} %bitcast.282, bf16[1280,16,64]{0,2,1:T(8,128)(2,1)S(1)} %bitcast.276, pred[640,1280]{1,0:T(8,128)(4,1)S(1)} %and_or_fusion), kind=kOutput, calls=%fused_computation.170 | convolution fusion | flops 1717032960 | bytes 57221120 | tf_op jit(solution)/shard_map/while/body/eval_jaxpr/qhd,khd->hqk/dot_general | solution.py:127
  343.7 17.2 fusion
  365.3 20.9 %fusion.54 = bf16[16,64,640]{2,1,0:T(8,128)(2,1)S(1)} fusion(bf16[1280,16,64]{0,2,1:T(8,128)(2,1)} %bitcast.287, f32[16,640,1280]{2,1,0:T(8,128)} %get-tuple-element.90, f32[16,640]{1,0:T(8,128)S(1)} %fusion, f32[16,640]{1,0:T(8,128)S(1)} %get-tuple-element.89), kind=kOutput, calls=%fused_computation.102 | convolution fusion | flops 1717698560 | bytes 56442880 | tf_op jit(solution)/shard_map/while/body/eval_jaxpr/hqk,khd->qhd/dot_general | solution.py:147
  392.0 19.0 %all-gather.22.cloned.1.call-done = bf16[1024,4096]{1,0:T(8,128)(2,1)} async-done(((bf16[64,4096]{1,0:T(8,128)(2,1)}), bf16[1024,4096]{1,0:T(8,128)(2,1)}) %all-gather.22.cloned.1.call-update) | async-done | bytes 8388624 | tf_op jit(solution)/shard_map/all_gather | solution.py:82
  411.0 32.4 %fusion.6 = (f32[640,4096]{1,0:T(8,128)}, f32[640,4096]{1,0:T(8,128)}) fusion(bf16[1024,4096]{1,0:T(8,128)(2,1)} %all-gather.22.cloned.1.call-done, f32[1024]{0:T(1024)S(1)} %bitcast.328, f32[640]{0:T(1024)S(1)} %fusion.80, f32[1,640,1024]{2,1,0:T(8,128)} %copy-done.6, f32[640]{0:T(1024)S(1)} %broadcast_multiply_fusion, f32[1024]{0:T(1024)S(1)} %bitcast.308), kind=kOutput, calls=%fused_computation.13 | convolution fusion | flops 5534515200 | bytes 31994880 | tf_op jit(solution)/shard_map/dot_general | solution.py:162
  443.4 43.0 %all-gather.24.cloned.1.call-done = bf16[4096,1024]{1,0:T(8,128)(2,1)} async-done(((bf16[256,1024]{1,0:T(8,128)(2,1)}), bf16[4096,1024]{1,0:T(8,128)(2,1)}) %all-gather.24.cloned.1.call-update) | async-done | bytes 8388624 | tf_op jit(solution)/shard_map/all_gather | solution.py:83
  486.3 16.7 add_convert_fusion
  521.6 38.6 %multiply_reduce_fusion = (f32[16,640]{1,0:T(8,128)S(1)}, f32[16,640,1280]{2,1,0:T(8,128)}) fusion(f32[16,640,1280]{2,1,0:T(8,128)} %get-tuple-element.90, f32[16,640]{1,0:T(8,128)S(1)} %log_add_fusion, bf16[640,16,64]{0,2,1:T(8,128)(2,1)S(1)} %bitcast.285, bf16[1280,16,64]{0,2,1:T(8,128)(2,1)} %bitcast.288), kind=kOutput, calls=%fused_computation.1 | convolution fusion | flops 1717032960 | bytes 108871680 | tf_op jit(solution)/shard_map/while/body/eval_jaxpr/qhd,khd->hqk/dot_general | solution.py:191
  560.2 42.2 %multiply_convert_fusion = bf16[16,640,1280]{2,1,0:T(8,128)(2,1)} fusion(f32[16,640,1280]{2,1,0:T(8,128)} %get-tuple-element.96, f32[16,640,1280]{2,1,0:T(8,128)} %get-tuple-element.90, f32[16,640]{1,0:T(8,128)S(1)} %get-tuple-element.95, f32[16,640]{1,0:T(8,128)S(1)} %log_add_fusion), kind=kLoop, calls=%fused_computation | loop fusion | flops 52428800 | bytes 131153920 | tf_op jit(solution)/shard_map/while/body/eval_jaxpr/convert_element_type | solution.py:195
  621.7 21.5 %fusion.36 = bf16[16,64,1280]{2,1,0:T(8,128)(2,1)} fusion(bf16[640,16,64]{0,2,1:T(8,128)(2,1)S(1)} %bitcast.286, f32[16,640,1280]{2,1,0:T(8,128)} %get-tuple-element.90, f32[16,640]{1,0:T(8,128)S(1)} %log_add_fusion), kind=kOutput, calls=%fused_computation.67 | convolution fusion | flops 1705246720 | bytes 56401920 | tf_op jit(solution)/shard_map/while/body/eval_jaxpr/hqk,qhd->khd/dot_general | solution.py:221
  653.5 14.9 multiply_convert_fusion.6
  677.9 19.7 %reduce-scatter.25.cloned.1.call-done = bf16[1,640,1024]{2,1,0:T(8,128)(2,1)} async-done(((bf16[1,1280,1024]{2,1,0:T(8,128)(2,1)}), bf16[1,640,1024]{2,1,0:T(8,128)(2,1)}) %reduce-scatter.25.cloned.1.call-update) | async-done | bytes 1310736 | tf_op jit(solution)/shard_map/reduce_scatter | solution.py:240
  764.6 24.6 %fusion.9 = bf16[4096,640]{0,1:T(8,128)(2,1)} fusion(f32[640,4096]{1,0:T(8,128)} %get-tuple-element.94), kind=kLoop, calls=%fused_computation.16 | loop fusion | flops 170393600 | bytes 15728640 | tf_op jit(solution)/shard_map/convert_element_type | solution.py:164
  824.8 34.0 %reduce-scatter.31.cloned.1.call-done = bf16[512,1024]{1,0:T(8,128)(2,1)} async-done(((bf16[1024,1024]{1,0:T(8,128)(2,1)}), bf16[512,1024]{1,0:T(8,128)(2,1)}) %reduce-scatter.31.cloned.1.call-update) | async-done | bytes 1048592 | tf_op jit(solution)/shard_map/reduce_scatter | solution.py:283
  858.8 56.4 %reduce-scatter.55.cloned.1.call-done = bf16[512,2048]{1,0:T(8,128)(2,1)} async-done(((bf16[1024,2048]{1,0:T(8,128)(2,1)}), bf16[512,2048]{1,0:T(8,128)(2,1)}) %reduce-scatter.55.cloned.1.call-update) | async-done | bytes 2097168 | tf_op jit(solution)/shard_map/reduce_scatter | solution.py:301
  915.3 56.5 %reduce-scatter.51.cloned.1.call-done = bf16[512,2048]{1,0:T(8,128)(2,1)} async-done(((bf16[1024,2048]{1,0:T(8,128)(2,1)}), bf16[512,2048]{1,0:T(8,128)(2,1)}) %reduce-scatter.51.cloned.1.call-update) | async-done | bytes 2097168 | tf_op jit(solution)/shard_map/reduce_scatter | solution.py:298
  971.9 101.5 %reduce-scatter.43.cloned.1.call-done = bf16[512,4096]{1,0:T(8,128)(2,1)} async-done(((bf16[1024,4096]{1,0:T(8,128)(2,1)}), bf16[512,4096]{1,0:T(8,128)(2,1)}) %reduce-scatter.43.cloned.1.call-update) | async-done | bytes 4194320 | tf_op jit(solution)/shard_map/reduce_scatter | solution.py:292
  1073.6 101.3 %reduce-scatter.47.cloned.1.call-done = bf16[2048,1024]{1,0:T(8,128)(2,1)} async-done(((bf16[4096,1024]{1,0:T(8,128)(2,1)}), bf16[2048,1024]{1,0:T(8,128)(2,1)}) %reduce-scatter.47.cloned.1.call-update) | async-done | bytes 4194320 | tf_op jit(solution)/shard_map/reduce_scatter | solution.py:295
  1188.1 46.0 %reduce-scatter.61.cloned.1.call-done = bf16[32,8]{1,0:T(8,128)(2,1)} async-done(((bf16[512,8]{1,0:T(8,128)(2,1)}), bf16[32,8]{1,0:T(8,128)(2,1)}) %reduce-scatter.61.cloned.1.call-update) | async-done | bytes 528
  1235.4 58.7 %reduce-scatter.41.cloned.1.call-done = bf16[32,1024]{1,0:T(8,128)(2,1)} async-done(((bf16[512,1024]{1,0:T(8,128)(2,1)}), bf16[32,1024]{1,0:T(8,128)(2,1)}) %reduce-scatter.41.cloned.1.call-update) | async-done | bytes 65552 | tf_op jit(solution)/shard_map/reduce_scatter | solution.py:328
  1295.7 59.0 %reduce-scatter.37.cloned.1.call-done = bf16[32,1024]{1,0:T(8,128)(2,1)} async-done(((bf16[512,1024]{1,0:T(8,128)(2,1)}), bf16[32,1024]{1,0:T(8,128)(2,1)}) %reduce-scatter.37.cloned.1.call-update) | async-done | bytes 65552 | tf_op jit(solution)/shard_map/reduce_scatter | solution.py:325
  1356.1 58.5 %reduce-scatter.29.cloned.1.call-done = bf16[32,1024]{1,0:T(8,128)(2,1)} async-done(((bf16[512,1024]{1,0:T(8,128)(2,1)}), bf16[32,1024]{1,0:T(8,128)(2,1)}) %reduce-scatter.29.cloned.1.call-update) | async-done | bytes 65552 | tf_op jit(solution)/shard_map/reduce_scatter | solution.py:319
  1416.1 59.0 %reduce-scatter.33.cloned.1.call-done = bf16[32,1024]{1,0:T(8,128)(2,1)} async-done(((bf16[512,1024]{1,0:T(8,128)(2,1)}), bf16[32,1024]{1,0:T(8,128)(2,1)}) %reduce-scatter.33.cloned.1.call-update) | async-done | bytes 65552 | tf_op jit(solution)/shard_map/reduce_scatter | solution.py:322
  1476.6 62.7 %reduce-scatter.57.cloned.1.call-done = bf16[32,2048]{1,0:T(8,128)(2,1)} async-done(((bf16[512,2048]{1,0:T(8,128)(2,1)}), bf16[32,2048]{1,0:T(8,128)(2,1)}) %reduce-scatter.57.cloned.1.call-update) | async-done | bytes 131088 | tf_op jit(solution)/shard_map/reduce_scatter | solution.py:340
  1540.9 63.0 %reduce-scatter.53.cloned.1.call-done = bf16[32,2048]{1,0:T(8,128)(2,1)} async-done(((bf16[512,2048]{1,0:T(8,128)(2,1)}), bf16[32,2048]{1,0:T(8,128)(2,1)}) %reduce-scatter.53.cloned.1.call-update) | async-done | bytes 131088 | tf_op jit(solution)/shard_map/reduce_scatter | solution.py:337
  1605.5 73.9 %reduce-scatter.45.cloned.1.call-done = bf16[32,4096]{1,0:T(8,128)(2,1)} async-done(((bf16[512,4096]{1,0:T(8,128)(2,1)}), bf16[32,4096]{1,0:T(8,128)(2,1)}) %reduce-scatter.45.cloned.1.call-update) | async-done | bytes 262160 | tf_op jit(solution)/shard_map/reduce_scatter | solution.py:331
  1681.2 74.0 %reduce-scatter.49.cloned.1.call-done = bf16[128,1024]{1,0:T(8,128)(2,1)} async-done(((bf16[2048,1024]{1,0:T(8,128)(2,1)}), bf16[128,1024]{1,0:T(8,128)(2,1)}) %reduce-scatter.49.cloned.1.call-update) | async-done | bytes 262160 | tf_op jit(solution)/shard_map/reduce_scatter | solution.py:334
  (244 shorter events, 261.2 us)
Async XLA Ops:
  7.2 56.3 %all-gather.12.cloned.1.call-start = ((), (), s32[]{:S(2)}) async-start(), calls=%async_computation.20 | async-start | bytes 4456448 | tf_op jit(solution)/shard_map/all_gather | solution.py:84
  7.9 97.6 %all-gather.18.cloned.1.call-start = ((), (), s32[]{:S(2)}) async-start(), calls=%async_computation.23 | async-start | bytes 2228224 | tf_op jit(solution)/shard_map/all_gather | solution.py:79
  8.7 139.3 %all-gather.14.cloned.1.call-start = ((), (), s32[]{:S(2)}) async-start(), calls=%async_computation.21 | async-start | bytes 2228224 | tf_op jit(solution)/shard_map/all_gather | solution.py:80
  9.4 303.5 %all-gather.16.cloned.1.call-start = ((), (), s32[]{:S(2)}) async-start(), calls=%async_computation.22 | async-start | bytes 2228224 | tf_op jit(solution)/shard_map/all_gather | solution.py:78
  10.0 307.8 %all-gather.28.cloned.1.call-start = ((), (), s32[]{:S(2)}) async-start(), calls=%async_computation.47 | async-start | bytes 3932160 | tf_op jit(solution)/shard_map/all_gather | solution.py:121
  109.9 251.0 %all-gather.26.cloned.1.call-start = ((), (), s32[]{:S(2)}) async-start(), calls=%async_computation.46 | async-start | bytes 3932160 | tf_op jit(solution)/shard_map/all_gather | solution.py:122
  152.2 234.1 %all-gather.20.cloned.1.call-start = ((), (), s32[]{:S(2)}) async-start(), calls=%async_computation.24 | async-start | bytes 2228224 | tf_op jit(solution)/shard_map/all_gather | solution.py:81
  153.0 258.0 %all-gather.22.cloned.1.call-start = ((), (), s32[]{:S(2)}) async-start(), calls=%async_computation.25 | async-start | bytes 8912896 | tf_op jit(solution)/shard_map/all_gather | solution.py:82
  153.7 332.6 %all-gather.24.cloned.1.call-start = ((), (), s32[]{:S(2)}) async-start(), calls=%async_computation.26 | async-start | bytes 8912896 | tf_op jit(solution)/shard_map/all_gather | solution.py:83
  161.2 14.3 collective-permute-start.1
  175.6 33.9 %collective-permute-start.2 = (bf16[256,2048]{1,0:T(8,128)(2,1)S(1)}, bf16[256,2048]{1,0:T(8,128)(2,1)S(1)}, u32[]{:S(2)}, u32[]{:S(2)}) collective-permute-start(bf16[256,2048]{1,0:T(8,128)(2,1)S(1)} %pad_maximum_fusion.1), channel_id=1, source_target_pairs={{0,24},{2,26},{4,28},{6,30},{8,0},{10,2},{12,4},{14,6},{16,8},{18,... | collective-permute-start | bytes 3145736 | tf_op jit(solution)/shard_map/ppermute | solution.py:20
  210.9 93.3 %collective-permute-start.3 = (bf16[512,2048]{1,0:T(8,128)(2,1)}, bf16[512,2048]{1,0:T(8,128)(2,1)}, u32[]{:S(2)}, u32[]{:S(2)}) collective-permute-start(bf16[512,2048]{1,0:T(8,128)(2,1)} %pad_maximum_fusion), channel_id=1, source_target_pairs={{0,16},{2,18},{4,20},{6,22},{8,24},{10,26},{12,28},{14,30},{16,0},... | collective-permute-start | bytes 6291464 | tf_op jit(solution)/shard_map/ppermute | solution.py:20
  211.5 462.0 %reduce-scatter.23.cloned.1.call-start = ((), (), s32[]{:S(2)}) async-start(), calls=%async_computation.27 | async-start | bytes 3932160 | tf_op jit(solution)/shard_map/reduce_scatter | solution.py:237
  621.6 76.0 %reduce-scatter.25.cloned.1.call-start = ((), (), s32[]{:S(2)}) async-start(), calls=%async_computation.28 | async-start | bytes 3932160 | tf_op jit(solution)/shard_map/reduce_scatter | solution.py:240
  647.7 169.9 %reduce-scatter.59.cloned.1.call-start = ((), (), s32[]{:S(2)}) async-start(), calls=%async_computation.45 | async-start | bytes 24576 | tf_op jit(solution)/shard_map/reduce_scatter | solution.py:304
  712.6 106.6 %reduce-scatter.39.cloned.1.call-start = ((), (), s32[]{:S(2)}) async-start(), calls=%async_computation.35 | async-start | bytes 3145728 | tf_op jit(solution)/shard_map/reduce_scatter | solution.py:289
  718.1 101.9 %reduce-scatter.35.cloned.1.call-start = ((), (), s32[]{:S(2)}) async-start(), calls=%async_computation.33 | async-start | bytes 3145728 | tf_op jit(solution)/shard_map/reduce_scatter | solution.py:286
  729.1 95.6 %reduce-scatter.27.cloned.1.call-start = ((), (), s32[]{:S(2)}) async-start(), calls=%async_computation.29 | async-start | bytes 3145728 | tf_op jit(solution)/shard_map/reduce_scatter | solution.py:280
  732.7 126.0 %reduce-scatter.31.cloned.1.call-start = ((), (), s32[]{:S(2)}) async-start(), calls=%async_computation.31 | async-start | bytes 3145728 | tf_op jit(solution)/shard_map/reduce_scatter | solution.py:283
  736.6 178.7 %reduce-scatter.55.cloned.1.call-start = ((), (), s32[]{:S(2)}) async-start(), calls=%async_computation.43 | async-start | bytes 6291456 | tf_op jit(solution)/shard_map/reduce_scatter | solution.py:301
  743.2 228.6 %reduce-scatter.51.cloned.1.call-start = ((), (), s32[]{:S(2)}) async-start(), calls=%async_computation.41 | async-start | bytes 6291456 | tf_op jit(solution)/shard_map/reduce_scatter | solution.py:298
  743.8 329.5 %reduce-scatter.43.cloned.1.call-start = ((), (), s32[]{:S(2)}) async-start(), calls=%async_computation.37 | async-start | bytes 12582912 | tf_op jit(solution)/shard_map/reduce_scatter | solution.py:292
  764.5 410.4 %reduce-scatter.47.cloned.1.call-start = ((), (), s32[]{:S(2)}) async-start(), calls=%async_computation.39 | async-start | bytes 12582912 | tf_op jit(solution)/shard_map/reduce_scatter | solution.py:295
  817.6 416.5 %reduce-scatter.61.cloned.1.call-start = ((), (), s32[]{:S(2)}) async-start(), calls=%async_computation.48 | async-start | bytes 139264
  819.2 475.0 %reduce-scatter.41.cloned.1.call-start = ((), (), s32[]{:S(2)}) async-start(), calls=%async_computation.36 | async-start | bytes 1114112 | tf_op jit(solution)/shard_map/reduce_scatter | solution.py:328
  819.9 534.7 %reduce-scatter.37.cloned.1.call-start = ((), (), s32[]{:S(2)}) async-start(), calls=%async_computation.34 | async-start | bytes 1114112 | tf_op jit(solution)/shard_map/reduce_scatter | solution.py:325
  820.6 594.0 %reduce-scatter.29.cloned.1.call-start = ((), (), s32[]{:S(2)}) async-start(), calls=%async_computation.30 | async-start | bytes 1114112 | tf_op jit(solution)/shard_map/reduce_scatter | solution.py:319
  824.7 650.4 %reduce-scatter.33.cloned.1.call-start = ((), (), s32[]{:S(2)}) async-start(), calls=%async_computation.32 | async-start | bytes 1114112 | tf_op jit(solution)/shard_map/reduce_scatter | solution.py:322
  858.8 680.5 %reduce-scatter.57.cloned.1.call-start = ((), (), s32[]{:S(2)}) async-start(), calls=%async_computation.44 | async-start | bytes 2228224 | tf_op jit(solution)/shard_map/reduce_scatter | solution.py:340
  915.2 688.7 %reduce-scatter.53.cloned.1.call-start = ((), (), s32[]{:S(2)}) async-start(), calls=%async_computation.42 | async-start | bytes 2228224 | tf_op jit(solution)/shard_map/reduce_scatter | solution.py:337
  971.8 707.6 %reduce-scatter.45.cloned.1.call-start = ((), (), s32[]{:S(2)}) async-start(), calls=%async_computation.38 | async-start | bytes 4456448 | tf_op jit(solution)/shard_map/reduce_scatter | solution.py:331
  1073.4 681.8 %reduce-scatter.49.cloned.1.call-start = ((), (), s32[]{:S(2)}) async-start(), calls=%async_computation.40 | async-start | bytes 4456448 | tf_op jit(solution)/shard_map/reduce_scatter | solution.py:334
  (39 other events, 2901.6 us)
Sparse Core Ops, SparseCore 0:
  10.2 53.2 all-gather.11
  65.7 39.8 all-gather.17
  107.7 40.1 all-gather.13
  150.0 52.2 all-gather.15
  203.7 46.1 all-gather.27
  251.8 39.0 all-gather.25
  293.1 42.0 all-gather.19
  337.3 73.6 all-gather.21
  413.2 73.1 all-gather.23
  621.7 35.8 reduce-scatter.22
  659.9 37.5 reduce-scatter.24
  712.8 9.7 reduce-scatter.58
  724.8 31.8 reduce-scatter.38
  758.9 31.8 reduce-scatter.34
  792.8 31.8 reduce-scatter.26
  826.9 31.8 reduce-scatter.30
  860.9 54.3 reduce-scatter.54
  917.5 54.2 reduce-scatter.50
  974.1 99.2 reduce-scatter.42
  1075.6 99.2 reduce-scatter.46
  1178.9 55.0 reduce-scatter.60
  1237.7 56.4 reduce-scatter.40
  1298.2 56.3 reduce-scatter.36
  1358.1 56.4 reduce-scatter.28
  1418.7 56.3 reduce-scatter.32
  1478.7 60.5 reduce-scatter.56
  1543.3 60.5 reduce-scatter.52
  1607.8 71.5 reduce-scatter.44
  1683.8 71.3 reduce-scatter.48
